TPU v7x, 32 devices: a whole 2x2x4 slice. The times are simulated.
32 devices in a mesh: col: 4 (over y, x), row: 8 (over z, core).
Axes of the slice: x: 2, y: 2, z: 4, core: 2. Of those that a mesh axis runs over, the one named last changes fastest.
Arguments:
- upper_blocks: float32 [4096, 512], P('row', 'col'), may hold values from -40 to 40
- lower_blocks: float32 [4096, 512], P('row', 'col'), may hold values from -40 to 40
Outputs:
- upper_rotated: float32 [4096, 512], P('row', 'col')
- lower_rotated: float32 [4096, 512], P('row', 'col')
All inputs are finite; a program needn't handle non-finite values.
Results may differ from a plain program's by a relative error of at most 0.0001.
Values sent between devices are 32-bit elements; how exact they have to be, the bound alone decides.
A program may use at most 64 MiB of HBM per device.

v0:
```python
import functools

import jax
import jax.numpy as jnp
from jax import lax
from jax.experimental import pallas as pl
from jax.experimental.pallas import tpu as pltpu
from jax.sharding import PartitionSpec as P

ROUNDS = 2
LOADS = 2
SWAPS = 2
SHIFTS = 4
STORES = 4
MESH = pl.DeviceIdType.MESH
F32 = jnp.float32
BF16 = jnp.bfloat16


def split(x):
    high = x.astype(BF16)
    low = (x - high.astype(F32)).astype(BF16)
    return high, low


def split_three(x):
    high = x.astype(BF16)
    rest = x - high.astype(F32)
    middle = rest.astype(BF16)
    return high, middle, (rest - middle.astype(F32)).astype(BF16)


def fast_dot(a, b):
    return jnp.dot(a, b, preferred_element_type=F32)


def exact_dot(a, b):
    width = b.shape[1]
    (a0, a1, a2), (b0, b1, b2) = split_three(a), split_three(b)
    upper = jnp.concatenate([b0, b1], axis=1)
    lower = jnp.concatenate([b1, b0], axis=1)
    large = fast_dot(jnp.concatenate([a0, a1], axis=1), jnp.concatenate([upper, lower], axis=0))
    small = fast_dot(jnp.concatenate([a0, a2], axis=1), jnp.concatenate([b2, b0], axis=0))
    return large[:, :width] + (large[:, width:] + small)


def gram(upper, lower):
    width = upper.shape[1]
    left = jnp.concatenate(split(upper), axis=1)
    right = jnp.concatenate(split(lower), axis=1)
    q = lax.dot_general(
        left, right, (((0,), (0,)), ((), ())), preferred_element_type=F32
    )
    return q[:width, :width] + (q[:width, width:] + q[width:, :width])


def step_count(width):
    square = (width / 4.0) ** 2
    spread = 0.5 * square / (1.0 + 0.5 * square)
    steps = 0
    while spread > 1e-3:
        spread = spread * spread / (2.0 - spread * spread)
        steps += 1
    return steps


def rotation(p):
    width = p.shape[0]
    rows = lax.broadcasted_iota(jnp.int32, (width, width), 0)
    lanes = lax.broadcasted_iota(jnp.int32, (width, width), 1)
    eye = (rows == lanes).astype(F32)
    s = exact_dot(p, p.T)
    total = jnp.sum(jnp.sum(p * p, axis=0, keepdims=True), axis=1, keepdims=True)
    total = jnp.broadcast_to(total, (1, width))
    scale = 1.0 / (1.0 + 0.5 * total)
    spread = 0.5 * total * scale
    e = spread * eye - scale * s
    x = None
    steps = step_count(width)
    for step in range(steps):
        square = spread * spread
        gain = 2.0 / (2.0 - square)
        spread = 0.5 * square * gain
        if step == 0:
            x = (gain * scale) * (eye + e)
            squared = exact_dot(e, e)
        elif step < steps - 1:
            squared = exact_dot(e, e)
            x = gain * (x + exact_dot(x, e))
        else:
            x = gain * (x + exact_dot(x, e))
        if step < steps - 1:
            e = gain * squared - spread * eye
    e = (eye - x) - exact_dot(s, x)
    x = x + exact_dot(x, e)
    ap = exact_dot(x, p)
    cross = 2.0 * ap
    keep_upper = 2.0 * x - eye
    keep_lower = eye - exact_dot(p.T, cross)
    top = jnp.concatenate([keep_upper, cross], axis=1)
    bottom = jnp.concatenate([-cross.T, keep_lower], axis=1)
    return jnp.concatenate([top, bottom], axis=0)


def turn(upper, lower, parts):
    high, low = split(jnp.concatenate([upper, lower], axis=1))
    w_high, w_low = parts
    return fast_dot(high, w_high) + (fast_dot(low, w_high) + fast_dot(high, w_low))


def kernel(
    n_row, n_col, upper_hbm, lower_hbm, work, out_p,
    loaded, swapped, gram_out, gram_in, line_out, line_in, pair,
    swap_send, swap_recv, gram_send, gram_recv, line_send, line_recv,
    pair_send, pair_recv, shift_send, shift_recv, load_sem,
):
    depth, width = upper_hbm.shape
    upper_ref, lower_ref = loaded.at[0], loaded.at[1]
    half = width // 2
    n_line = n_row // 2
    row_total = float(depth * n_row)
    row, col = lax.axis_index("row"), lax.axis_index("col")
    core = lax.rem(row, 2)
    chip_row = row - core
    partner = chip_row + 1 - core
    odd = lax.rem(col, 2)
    beside = col + 1 - 2 * odd
    ahead = lax.rem(col + 2, n_col)
    behind = lax.rem(col + n_col - 2, n_col)
    shift_to = ahead + odd * (behind - ahead)

    def line_row(k):
        return lax.rem(row + 2 * k, n_row)

    def piece(i, count):
        return pl.ds(i * (depth // count), depth // count)

    loads = []
    for i in range(LOADS):
        rows = piece(i, LOADS)
        for which, ref in enumerate((upper_hbm, lower_hbm)):
            loads.append(pltpu.make_async_copy(ref.at[rows], loaded.at[which, rows], load_sem.at[which, i]))
            loads[-1].start()
    barrier = pltpu.get_barrier_semaphore()
    greeted = [(chip_row, beside), (chip_row + 1, beside), (partner, col)]
    greeted += [(line_row(k), col) for k in range(1, n_line)]
    greeted += [(row, ahead)] + ([] if n_col == 4 else [(row, behind)])
    for r, c in greeted:
        pl.semaphore_signal(barrier, inc=1, device_id={"row": r, "col": c}, device_id_type=MESH)

    def remote(src, dst, send, recv, r, c):
        return pltpu.make_async_remote_copy(
            src_ref=src, dst_ref=dst, send_sem=send, recv_sem=recv,
            device_id={"row": r, "col": c}, device_id_type=MESH,
        )

    def put_statistics(index, g, upper_sums, lower_sums):
        which = lax.broadcasted_iota(jnp.int32, (8, width), 0)
        norms = jnp.where(which == 0, upper_sums, jnp.where(which == 1, lower_sums, 0.0))
        for k in range(2):
            gram_out[index, k, :half, :] = g[k * half : (k + 1) * half]
            gram_out[index, k, half:, :] = norms

    def reduce_line(index, own):
        line_out[index] = own
        copies = []
        for k in range(1, n_line):
            copies.append(
                remote(
                    line_out.at[index], line_in.at[index, k - 1],
                    line_send.at[index, k - 1], line_recv.at[index, k - 1], line_row(k), col,
                )
            )
            copies[-1].start()
        total = own
        for k in range(1, n_line):
            copies[k - 1].wait_recv()
            total = total + line_in[index, k - 1]
        return total, copies

    def coupling(index, total):
        pair[index, core] = total[:half]
        copy = remote(
            pair.at[index, core], pair.at[index, core],
            pair_send.at[index], pair_recv.at[index], partner, col,
        )
        copy.start()
        norms = total[half:] / row_total
        a_row, b = norms[:1], norms[1:2]
        a = jnp.broadcast_to(a_row, (width, width)).T
        gap, both = a - b, a + b
        factor = -gap / (2.0 * gap * gap + 0.5 * both * both + 1e-05)
        copy.wait_recv()
        cross_gram = pair[index].reshape(width, width) / row_total
        return cross_gram * factor, copy

    pending = []

    def statistics(index, count, fetch):
        g, upper_sums, lower_sums = 0.0, 0.0, 0.0
        for i in range(count):
            upper, lower = fetch(i, piece(i, count))
            g = g + gram(upper, lower)
            upper_sums = upper_sums + jnp.sum(upper * upper, axis=0, keepdims=True)
            lower_sums = lower_sums + jnp.sum(lower * lower, axis=0, keepdims=True)
        put_statistics(index, g, upper_sums, lower_sums)

    def fetch_loaded(i, rows):
        loads[2 * i].wait()
        loads[2 * i + 1].wait()
        return loaded[0, rows, :], loaded[1, rows, :]

    statistics(0, LOADS, fetch_loaded)
    pl.semaphore_wait(barrier, len(greeted))

    copies = []
    for k in range(2):
        copies.append(
            remote(
                gram_out.at[0, k], gram_in.at[core], gram_send.at[k], gram_recv.at[core],
                chip_row + k, beside,
            )
        )
        copies[-1].start()
    pending += copies
    swaps = []
    for i in range(SWAPS):
        rows = piece(i, SWAPS)
        for which, ref in enumerate((upper_ref, lower_ref)):
            swaps.append(
                remote(
                    ref.at[rows], swapped.at[which, rows],
                    swap_send.at[which, i], swap_recv.at[which, i], row, beside,
                )
            )
            swaps[-1].start()
    pending += swaps
    for k in range(2):
        pltpu.make_async_remote_copy(
            src_ref=gram_out.at[0, k], dst_ref=gram_in.at[k], send_sem=gram_send.at[k],
            recv_sem=gram_recv.at[k], device_id={"row": row, "col": beside}, device_id_type=MESH,
        ).wait_recv()
    total, copies = reduce_line(0, gram_in[0] + gram_in[1])
    pending += copies
    p, copy = coupling(0, total)
    pending.append(copy)
    parts = split(rotation(p))

    shifts = []
    for i in range(SHIFTS):
        rows = piece(i, SHIFTS)
        if i % (SHIFTS // SWAPS) == 0:
            swaps[2 * (i * SWAPS // SHIFTS)].wait_recv()
            swaps[2 * (i * SWAPS // SHIFTS) + 1].wait_recv()
        y = turn(swapped[0, rows, :], swapped[1, rows, :], parts)
        work[0, rows, :] = y[:, :width]
        work[1, rows, :] = y[:, width:]
        shifts.append(
            remote(
                work.at[odd, rows], work.at[2, rows], shift_send.at[i], shift_recv.at[i],
                row, shift_to,
            )
        )
        shifts[-1].start()
    pending += shifts

    upper_slot, lower_slot = 2 - 2 * odd, 1 + odd

    def fetch_shifted(i, rows):
        shifts[i].wait_recv()
        return work[upper_slot, rows, :], work[lower_slot, rows, :]

    statistics(1, SHIFTS, fetch_shifted)
    copy = remote(
        gram_out.at[1, 1 - core], gram_in.at[2], gram_send.at[2], gram_recv.at[2], partner, col
    )
    copy.start()
    pending.append(copy)
    copy.wait_recv()
    total, copies = reduce_line(1, gram_out[1, core] + gram_in[2])
    pending += copies
    p, copy = coupling(1, total)
    pending.append(copy)
    out_p[...] = p
    for copy in pending:
        copy.wait_send()


def finish(work, p_ref, out_upper, out_lower, stage, sems):
    depth, width = out_upper.shape
    chunk = depth // STORES
    odd = lax.rem(lax.axis_index("col"), 2)
    upper_slot, lower_slot = 2 - 2 * odd, 1 + odd
    parts = split(rotation(p_ref[...]))
    copies = []
    for i in range(STORES):
        rows = pl.ds(i * chunk, chunk)
        y = turn(work[upper_slot, rows, :], work[lower_slot, rows, :], parts)
        for which, out in enumerate((out_upper, out_lower)):
            stage[which, rows, :] = y[:, which * width : (which + 1) * width]
            copies.append(pltpu.make_async_copy(stage.at[which, rows], out.at[rows], sems.at[which, i]))
            copies[-1].start()
    for copy in copies:
        copy.wait()


def shards(n_row, n_col, upper_blocks, lower_blocks):
    depth, width = upper_blocks.shape
    half = width // 2
    n_line = n_row // 2
    out = jax.ShapeDtypeStruct((depth, width), F32)
    dma = pltpu.SemaphoreType.DMA
    work, p = pl.pallas_call(
        functools.partial(kernel, n_row, n_col),
        out_shape=(pltpu.VMEM((3, depth, width), F32), pltpu.VMEM((width, width), F32)),
        in_specs=[pl.BlockSpec(memory_space=pl.ANY)] * 2,
        out_specs=(pl.BlockSpec(memory_space=pltpu.VMEM),) * 2,
        scratch_shapes=[
            pltpu.VMEM((2, depth, width), F32),
            pltpu.VMEM((2, depth, width), F32),
            pltpu.VMEM((ROUNDS, 2, half + 8, width), F32),
            pltpu.VMEM((3, half + 8, width), F32),
            pltpu.VMEM((ROUNDS, half + 8, width), F32),
            pltpu.VMEM((ROUNDS, n_line - 1, half + 8, width), F32),
            pltpu.VMEM((ROUNDS, 2, half, width), F32),
            dma((2, SWAPS)),
            dma((2, SWAPS)),
            dma((3,)),
            dma((3,)),
            dma((ROUNDS, n_line - 1)),
            dma((ROUNDS, n_line - 1)),
            dma((ROUNDS,)),
            dma((ROUNDS,)),
            dma((SHIFTS,)),
            dma((SHIFTS,)),
            dma((2, LOADS)),
        ],
        compiler_params=pltpu.CompilerParams(collective_id=0, has_side_effects=True),
    )(upper_blocks, lower_blocks)
    return pl.pallas_call(
        finish,
        out_shape=(out, out),
        in_specs=[pl.BlockSpec(memory_space=pltpu.VMEM)] * 2,
        out_specs=(pl.BlockSpec(memory_space=pl.ANY),) * 2,
        scratch_shapes=[pltpu.VMEM((2, depth, width), F32), dma((2, STORES))],
    )(*(pltpu.with_memory_space_constraint(x, pltpu.VMEM) for x in (work, p)))


def solution(mesh):
    placed = (P("row", "col"), P("row", "col"))
    return jax.shard_map(
        functools.partial(shards, mesh.shape["row"], mesh.shape["col"]),
        mesh=mesh,
        in_specs=placed,
        out_specs=(P("row", "col"), P("row", "col")),
        check_vma=False,
    )
```

profile of v0, /device:TPU:1, one launch (start us, length us, event | category | flops | bytes accessed | tf_op | source)
XLA Modules:
  0.0 36.6 jit_solution(8773783502434847293)
XLA Ops:
  0.6 32.6 %shard_map.41 = (f32[3,512,128]{2,1,0:T(8,128)S(1)}, f32[128,128]{1,0:T(8,128)S(1)}) custom-call(f32[512,128]{1,0:T(8,128)} %upper_hbm.1, f32[512,128]{1,0:T(8,128)} %lower_hbm.1), custom_call_target="tpu_custom_call" | custom-call | tf_op jit(solution)/shard_map/pallas_call | solution.py:313
  33.2 3.4 %shard_map.42 = (f32[512,128]{1,0:T(8,128)}, f32[512,128]{1,0:T(8,128)}) custom-call(f32[3,512,128]{2,1,0:T(8,128)S(1)} %get-tuple-element.4.work, f32[128,128]{1,0:T(8,128)S(1)} %get-tuple-element.5.p_ref), custom_call_target="tpu_custom_call" | custom-call | tf_op jit(solution)/shard_map/pallas_call | solution.py:340
where the time goes:
time: 36.9 us; the launch traced here: 36.6 us
  Pallas kernels  36 us (98%)
  between operations  0.64 us (2%)
    pallas_call x1, Pallas kernels, shards(): pl.pallas_call(functools.partial(kernel, n_row, n_col), out_shape=(pltpu....  32.6 us
    pallas_call x1, Pallas kernels, shards(): pl.pallas_call(finish, out_shape=(out, out), in_specs=[pl.BlockSpec(memor...  3.36 us

commit v1 on v0

v1 whole, which is shorter than its diff:
```python
import functools

import jax
import jax.numpy as jnp
from jax import lax
from jax.experimental import pallas as pl
from jax.experimental.pallas import tpu as pltpu
from jax.sharding import PartitionSpec as P

ROUNDS = 2
LOADS = 2
SWAPS = 8
EARLY = 1
RELAYS = 4
RELAYS_FIRST = 3
SHIFTS = 4
STORES = 4
MESH = pl.DeviceIdType.MESH
F32 = jnp.float32
BF16 = jnp.bfloat16


def split(x):
    high = x.astype(BF16)
    low = (x - high.astype(F32)).astype(BF16)
    return high, low


def split_three(x):
    high = x.astype(BF16)
    rest = x - high.astype(F32)
    middle = rest.astype(BF16)
    return high, middle, (rest - middle.astype(F32)).astype(BF16)


def fast_dot(a, b):
    return jnp.dot(a, b, preferred_element_type=F32)


def exact_dot(a, b):
    width = b.shape[1]
    (a0, a1, a2), (b0, b1, b2) = split_three(a), split_three(b)
    upper = jnp.concatenate([b0, b1], axis=1)
    lower = jnp.concatenate([b1, b0], axis=1)
    large = fast_dot(jnp.concatenate([a0, a1], axis=1), jnp.concatenate([upper, lower], axis=0))
    small = fast_dot(jnp.concatenate([a0, a2], axis=1), jnp.concatenate([b2, b0], axis=0))
    return large[:, :width] + (large[:, width:] + small)


def wide(b):
    both = jnp.concatenate(split(b), axis=1)
    return jnp.concatenate([both, both], axis=0)


def tall_dot(a, b_wide):
    width = a.shape[1]
    y = fast_dot(jnp.concatenate(split(a), axis=1), b_wide)
    return y[:, :width] + y[:, width:]


def gram(upper, lower):
    width = upper.shape[1]
    left = jnp.concatenate(split(upper), axis=1)
    right = jnp.concatenate(split(lower), axis=1)
    q = lax.dot_general(
        left, right, (((0,), (0,)), ((), ())), preferred_element_type=F32
    )
    return q[:width, :width] + (q[:width, width:] + q[width:, :width])


def identity(width):
    rows = lax.broadcasted_iota(jnp.int32, (width, width), 0)
    lanes = lax.broadcasted_iota(jnp.int32, (width, width), 1)
    return (rows == lanes).astype(F32)


def shrink(spread):
    square = spread * spread
    gain = 2.0 / (2.0 - square)
    return gain, 0.5 * square * gain


def step_count(width):
    square = (width / 4.0) ** 2
    spread = 0.5 * square / (1.0 + 0.5 * square)
    steps = 0
    while spread > 3e-6:
        spread = shrink(spread)[1]
        steps += 1
    return steps


def inverse(p):
    width = p.shape[0]
    eye = identity(width)
    s = exact_dot(p, p.T)
    total = jnp.sum(jnp.sum(p * p, axis=0, keepdims=True), axis=1, keepdims=True)
    total = jnp.broadcast_to(total, (1, width))
    scale = 1.0 / (1.0 + 0.5 * total)
    spread = 0.5 * total * scale
    e = spread * eye - scale * s
    x = None
    steps = step_count(width)
    for step in range(steps):
        gain, spread = shrink(spread)
        if step == 0:
            x = (gain * scale) * (eye + e)
        else:
            x = gain * (x + exact_dot(x, e))
        if step < steps - 1:
            e = gain * exact_dot(e, e) - spread * eye
    return x


def inverse_adaptive(p):
    width = p.shape[0]
    eye = identity(width)
    s = exact_dot(p, p.T)
    bound = 1.0001 * jnp.max(jnp.sum(jnp.abs(s), axis=0, keepdims=True))
    scale = 1.0 / (1.0 + 0.5 * bound)
    spread = 0.5 * bound * scale
    e = spread * eye - scale * s
    gain, spread = shrink(spread)
    x = (gain * scale) * (eye + e)
    squared = exact_dot(e, e)

    def body(state):
        x, squared, gain, spread = state
        e = gain * squared - spread * eye
        gain, spread = shrink(spread)
        return gain * (x + exact_dot(x, e)), exact_dot(e, e), gain, spread

    return lax.while_loop(lambda state: state[3] > 3e-6, body, (x, squared, gain, spread))[0]


def turn(upper, lower, x_wide, p_wide, d):
    v = tall_dot(d, x_wide)
    return v - upper, lower + tall_dot(v, p_wide)


def kernel(
    n_row, n_col, upper_hbm, lower_hbm, work, out_p,
    loaded, swapped, relayed, gram_out, gram_in, line_out, line_in, totals, others,
    swap_send, swap_recv, gram_send, gram_recv, line_send, line_recv,
    pair_send, pair_recv, other_send, other_recv, relay_send, relay_recv,
    shift_send, shift_recv, load_sem, up_sem, down_sem,
):
    depth, width = upper_hbm.shape
    half = width // 2
    n_line = n_row // 2
    row_total = float(depth * n_row)
    row, col = lax.axis_index("row"), lax.axis_index("col")
    core = lax.rem(row, 2)
    chip_row = row - core
    place = chip_row // 2
    partner = chip_row + 1 - core
    odd = lax.rem(col, 2)
    beside = col + 1 - 2 * odd
    ahead = lax.rem(col + 2, n_col)
    behind = lax.rem(col + n_col - 2, n_col)
    shift_to = ahead + odd * (behind - ahead)
    has_prev, has_next = place > 0, place < n_line - 1

    def line_row(k):
        return lax.rem(row + 2 * k, n_row)

    def piece(i, count):
        return pl.ds(i * (depth // count), depth // count)

    loads = []
    for i in range(LOADS):
        rows = piece(i, LOADS)
        for which, ref in enumerate((upper_hbm, lower_hbm)):
            loads.append(pltpu.make_async_copy(ref.at[rows], loaded.at[which, rows], load_sem.at[which, i]))
            loads[-1].start()
    barrier = pltpu.get_barrier_semaphore()

    def greet(r, c):
        pl.semaphore_signal(barrier, inc=1, device_id={"row": r, "col": c}, device_id_type=MESH)

    greeted = [(chip_row, beside), (chip_row + 1, beside), (partner, col)]
    for c in [ahead] + ([] if n_col == 4 else [behind]):
        greeted += [(chip_row, c), (chip_row + 1, c)]
    for r, c in greeted:
        greet(r, c)

    @pl.when(has_prev)
    def _():
        greet(row - 2, col)

    @pl.when(has_next)
    def _():
        greet(row + 2, col)

    pl.semaphore_wait(barrier, len(greeted) + has_prev.astype(jnp.int32) + has_next.astype(jnp.int32))

    def remote(src, dst, send, recv, r, c):
        return pltpu.make_async_remote_copy(
            src_ref=src, dst_ref=dst, send_sem=send, recv_sem=recv,
            device_id={"row": r, "col": c}, device_id_type=MESH,
        )

    pending = []

    def start(copy):
        copy.start()
        pending.append(copy)
        return copy

    def start_swap(i, refs):
        rows = piece(i, SWAPS)
        return [
            start(
                remote(
                    ref.at[rows], swapped.at[which, rows],
                    swap_send.at[which, i], swap_recv.at[which, i], row, beside,
                )
            )
            for which, ref in enumerate(refs)
        ]

    swaps = [start_swap(i, (upper_hbm, lower_hbm)) for i in range(EARLY)]

    def put_statistics(index, g, upper_sums, lower_sums):
        which = lax.broadcasted_iota(jnp.int32, (8, width), 0)
        norms = jnp.where(which == 0, upper_sums, jnp.where(which == 1, lower_sums, 0.0))
        for k in range(2):
            gram_out[index, k, :half, :] = g[k * half : (k + 1) * half]
            gram_out[index, k, half:, :] = norms

    def reduce_line(index, own):
        line_out[index] = own
        copies = []
        for k in range(1, n_line):
            copies.append(
                start(
                    remote(
                        line_out.at[index], line_in.at[index, k - 1],
                        line_send.at[index, k - 1], line_recv.at[index, k - 1], line_row(k), col,
                    )
                )
            )

        def finish_line():
            total = own
            for k in range(1, n_line):
                copies[k - 1].wait_recv()
                total = total + line_in[index, k - 1]
            return total

        return finish_line

    def pair_copy(index):
        return remote(
            totals.at[index, core], totals.at[index, core],
            pair_send.at[index], pair_recv.at[index], partner, col,
        )

    def coupling(both_halves, norm_rows):
        norms = norm_rows / row_total
        a_row, b = norms[:1], norms[1:2]
        a = jnp.broadcast_to(a_row, (width, width)).T
        gap, both = a - b, a + b
        factor = -gap / (2.0 * gap * gap + 0.5 * both * both + 1e-05)
        return (both_halves.reshape(width, width) / row_total) * factor

    def statistics(index, pieces, fetch):
        g, upper_sums, lower_sums = 0.0, 0.0, 0.0
        for i, rows in enumerate(pieces):
            upper, lower = fetch(i, rows)
            g = g + gram(upper, lower)
            upper_sums = upper_sums + jnp.sum(upper * upper, axis=0, keepdims=True)
            lower_sums = lower_sums + jnp.sum(lower * lower, axis=0, keepdims=True)
        put_statistics(index, g, upper_sums, lower_sums)

    def fetch_loaded(i, rows):
        loads[2 * i].wait()
        loads[2 * i + 1].wait()
        return loaded[0, rows, :], loaded[1, rows, :]

    statistics(0, [piece(i, LOADS) for i in range(LOADS)], fetch_loaded)

    for k in range(2):
        start(
            remote(
                gram_out.at[0, k], gram_in.at[core], gram_send.at[k], gram_recv.at[core],
                chip_row + k, beside,
            )
        )
    swaps += [start_swap(i, (loaded.at[0], loaded.at[1])) for i in range(EARLY, SWAPS)]

    for s in range(n_line - 2):
        tell_up = jnp.logical_and(has_next, place > s)
        tell_down = jnp.logical_and(has_prev, place < n_line - 1 - s)

        @pl.when(tell_up)
        def _():
            pl.semaphore_signal(up_sem.at[s], inc=1, device_id={"row": row + 2, "col": col}, device_id_type=MESH)

        @pl.when(tell_down)
        def _():
            pl.semaphore_signal(down_sem.at[s], inc=1, device_id={"row": row - 2, "col": col}, device_id_type=MESH)

        @pl.when(place > s + 1)
        def _():
            pl.semaphore_wait(up_sem.at[s], 1)

        @pl.when(place < n_line - 2 - s)
        def _():
            pl.semaphore_wait(down_sem.at[s], 1)

    for k in range(2):
        remote(
            gram_out.at[0, k], gram_in.at[k], gram_send.at[k], gram_recv.at[k], row, beside
        ).wait_recv()
    finish_line = reduce_line(0, gram_in[0] + gram_in[1])

    relays = []

    def relay(i):
        rows = piece(i, SWAPS)
        for which in range(2):
            swaps[i][which].wait_recv()
            relays.append(
                start(
                    remote(
                        swapped.at[which, rows], relayed.at[which, rows],
                        relay_send.at[which, i], relay_recv.at[which, i], row, shift_to,
                    )
                )
            )

    for i in range(RELAYS_FIRST):
        relay(i)
    totals[0, core] = finish_line()
    own_copy = start(pair_copy(0))
    for k in range(2):
        start(
            remote(
                totals.at[0, core], others.at[core], other_send.at[k], other_recv.at[core],
                chip_row + k, shift_to,
            )
        )
    for i in range(RELAYS_FIRST, RELAYS):
        relay(i)
    own_copy.wait_recv()
    p = coupling(totals[0, :, :half, :], totals[0, 0, half:, :])
    early_rows = pl.ds(0, RELAYS * (depth // SWAPS))
    back = wide(p.T)
    d = swapped[0, early_rows, :] - tall_dot(swapped[1, early_rows, :], back)
    x_wide, p_wide = wide(2.0 * inverse(p)), wide(p)
    upper_slot, lower_slot = 2 - 2 * odd, 1 + odd

    late = depth - RELAYS * (depth // SWAPS)
    shifts = []
    shift_rows = []
    ready = RELAYS
    for i in range(SHIFTS):
        rows = pl.ds(depth - late + i * (late // SHIFTS), late // SHIFTS)
        shift_rows.append(rows)
        while ready * (depth // SWAPS) < depth - late + (i + 1) * (late // SHIFTS):
            swaps[ready][0].wait_recv()
            swaps[ready][1].wait_recv()
            ready += 1
        upper, lower = swapped[0, rows, :], swapped[1, rows, :]
        new_upper, new_lower = turn(upper, lower, x_wide, p_wide, upper - tall_dot(lower, back))
        work[upper_slot, rows, :] = new_upper
        work[lower_slot, rows, :] = new_lower
        shifts.append(
            start(
                remote(
                    work.at[2, rows], work.at[odd, rows], shift_send.at[i], shift_recv.at[i],
                    row, shift_to,
                )
            )
        )
    if RELAYS:
        upper, lower = swapped[0, early_rows, :], swapped[1, early_rows, :]
        new_upper, new_lower = turn(upper, lower, x_wide, p_wide, d)
        work[upper_slot, early_rows, :] = new_upper
        work[lower_slot, early_rows, :] = new_lower
        for k in range(2):
            remote(
                totals.at[0, k], others.at[k], other_send.at[k], other_recv.at[k], row, shift_to
            ).wait_recv()
        p = coupling(others[:, :half, :], others[0, half:, :])
        for copy in relays:
            copy.wait_recv()
        upper, lower = relayed[0], relayed[1]
        d = upper - tall_dot(lower, wide(p.T))
        new_upper, new_lower = turn(upper, lower, wide(2.0 * inverse(p)), wide(p), d)
        work[2 * odd, early_rows, :] = new_upper
        work[2 - odd, early_rows, :] = new_lower

    def fetch_shifted(i, rows):
        if i >= len(pieces) - SHIFTS:
            shifts[i - (len(pieces) - SHIFTS)].wait_recv()
        return work[0, rows, :], work[1, rows, :]

    pieces = ([early_rows] if RELAYS else []) + shift_rows
    statistics(1, pieces, fetch_shifted)
    copy = start(
        remote(gram_out.at[1, 1 - core], gram_in.at[2], gram_send.at[2], gram_recv.at[2], partner, col)
    )
    copy.wait_recv()
    total = reduce_line(1, gram_out[1, core] + gram_in[2])()
    totals[1, core] = total
    copy = start(pair_copy(1))
    copy.wait_recv()
    out_p[...] = coupling(totals[1, :, :half, :], totals[1, 0, half:, :])
    for copy in pending:
        copy.wait_send()


def finish(work, p_ref, out_upper, out_lower, stage, sems):
    depth, width = out_upper.shape
    chunk = depth // STORES
    p = p_ref[...]
    d = work[0] - tall_dot(work[1], wide(p.T))
    p_wide, x_wide = wide(p), wide(2.0 * inverse_adaptive(p))
    copies = []
    for i in range(STORES):
        rows = pl.ds(i * chunk, chunk)
        y = turn(work[0, rows, :], work[1, rows, :], x_wide, p_wide, d[i * chunk : (i + 1) * chunk])
        for which, out in enumerate((out_upper, out_lower)):
            stage[which, rows, :] = y[which]
            copies.append(pltpu.make_async_copy(stage.at[which, rows], out.at[rows], sems.at[which, i]))
            copies[-1].start()
    for copy in copies:
        copy.wait()


def shards(n_row, n_col, upper_blocks, lower_blocks):
    depth, width = upper_blocks.shape
    half = width // 2
    n_line = n_row // 2
    out = jax.ShapeDtypeStruct((depth, width), F32)
    dma = pltpu.SemaphoreType.DMA
    flag = pltpu.SemaphoreType.REGULAR
    work, p = pl.pallas_call(
        functools.partial(kernel, n_row, n_col),
        out_shape=(pltpu.VMEM((3, depth, width), F32), pltpu.VMEM((width, width), F32)),
        in_specs=[pl.BlockSpec(memory_space=pl.ANY)] * 2,
        out_specs=(pl.BlockSpec(memory_space=pltpu.VMEM),) * 2,
        scratch_shapes=[
            pltpu.VMEM((2, depth, width), F32),
            pltpu.VMEM((2, depth, width), F32),
            pltpu.VMEM((2, max(RELAYS, 1) * (depth // SWAPS), width), F32),
            pltpu.VMEM((ROUNDS, 2, half + 8, width), F32),
            pltpu.VMEM((3, half + 8, width), F32),
            pltpu.VMEM((ROUNDS, half + 8, width), F32),
            pltpu.VMEM((ROUNDS, n_line - 1, half + 8, width), F32),
            pltpu.VMEM((ROUNDS, 2, half + 8, width), F32),
            pltpu.VMEM((2, half + 8, width), F32),
            dma((2, SWAPS)),
            dma((2, SWAPS)),
            dma((3,)),
            dma((3,)),
            dma((ROUNDS, n_line - 1)),
            dma((ROUNDS, n_line - 1)),
            dma((ROUNDS,)),
            dma((ROUNDS,)),
            dma((2,)),
            dma((2,)),
            dma((2, max(RELAYS, 1))),
            dma((2, max(RELAYS, 1))),
            dma((SHIFTS,)),
            dma((SHIFTS,)),
            dma((2, LOADS)),
            flag((max(n_line - 2, 1),)),
            flag((max(n_line - 2, 1),)),
        ],
        compiler_params=pltpu.CompilerParams(collective_id=0, has_side_effects=True),
    )(upper_blocks, lower_blocks)
    return pl.pallas_call(
        finish,
        out_shape=(out, out),
        in_specs=[pl.BlockSpec(memory_space=pltpu.VMEM)] * 2,
        out_specs=(pl.BlockSpec(memory_space=pl.ANY),) * 2,
        scratch_shapes=[pltpu.VMEM((2, depth, width), F32), dma((2, STORES))],
    )(*(pltpu.with_memory_space_constraint(x, pltpu.VMEM) for x in (work, p)))


def solution(mesh):
    placed = (P("row", "col"), P("row", "col"))
    return jax.shard_map(
        functools.partial(shards, mesh.shape["row"], mesh.shape["col"]),
        mesh=mesh,
        in_specs=placed,
        out_specs=(P("row", "col"), P("row", "col")),
        check_vma=False,
    )
```

time: 36.9 us -> 35.1 us (0.951)
  Pallas kernels: 36 us -> 34.2 us
    pallas_call x1, Pallas kernels: 32.6 us -> 31.4 us  [shards(): pl.pallas_call(functools.partial(kernel, n_row, n_col), out_shape=(pltpu....]
    pallas_call x1, Pallas kernels: 3.36 us -> 2.75 us  [shards(): pl.pallas_call(finish, out_shape=(out, out), in_specs=[pl.BlockSpec(memor...]
where the time goes in v1:
time: 35.1 us; the launch traced here: 34.8 us
  Pallas kernels  34.2 us (97%)
  between operations  0.64 us (2%)
    pallas_call x1, Pallas kernels, shards(): pl.pallas_call(functools.partial(kernel, n_row, n_col), out_shape=(pltpu....  31.4 us
    pallas_call x1, Pallas kernels, shards(): pl.pallas_call(finish, out_shape=(out, out), in_specs=[pl.BlockSpec(memor...  2.75 us

profile of v1, /device:TPU:1, one launch (start us, length us, event | category | flops | bytes accessed | tf_op | source)
XLA Modules:
  0.0 34.8 jit_solution(7303345742326951723)
XLA Ops:
  0.6 31.4 %shard_map.41 = (f32[3,512,128]{2,1,0:T(8,128)S(1)}, f32[128,128]{1,0:T(8,128)S(1)}) custom-call(f32[512,128]{1,0:T(8,128)} %upper_hbm.1, f32[512,128]{1,0:T(8,128)} %lower_hbm.1), custom_call_target="tpu_custom_call" | custom-call | tf_op jit(solution)/shard_map/pallas_call | solution.py:440
  32.1 2.7 %shard_map.42 = (f32[512,128]{1,0:T(8,128)}, f32[512,128]{1,0:T(8,128)}) custom-call(f32[3,512,128]{2,1,0:T(8,128)S(1)} %get-tuple-element.4.work, f32[128,128]{1,0:T(8,128)S(1)} %get-tuple-element.5.p_ref), custom_call_target="tpu_custom_call" | custom-call | tf_op jit(solution)/shard_map/pallas_call | solution.py:475

commit v2 on v1

--- a/solution.py
+++ b/solution.py
@@ -9,11 +9,10 @@
 
 ROUNDS = 2
 LOADS = 2
-SWAPS = 8
-EARLY = 1
-RELAYS = 4
-RELAYS_FIRST = 3
-SHIFTS = 4
+RELAYED = 5
+SHIFTS = 3
+MOVES = 4
+MOVES_FIRST = 4
 STORES = 4
 MESH = pl.DeviceIdType.MESH
 F32 = jnp.float32
@@ -140,10 +139,10 @@
 
 def kernel(
     n_row, n_col, upper_hbm, lower_hbm, work, out_p,
-    loaded, swapped, relayed, gram_out, gram_in, line_out, line_in, totals, others,
-    swap_send, swap_recv, gram_send, gram_recv, line_send, line_recv,
+    loaded, relayed, home, gram_out, gram_in, line_out, line_in, totals, others,
+    gram_send, gram_recv, line_send, line_recv,
     pair_send, pair_recv, other_send, other_recv, relay_send, relay_recv,
-    shift_send, shift_recv, load_sem, up_sem, down_sem,
+    shift_send, shift_recv, move_send, move_recv, load_sem, up_sem, down_sem,
 ):
     depth, width = upper_hbm.shape
     half = width // 2
@@ -154,18 +153,21 @@
     chip_row = row - core
     place = chip_row // 2
     partner = chip_row + 1 - core
-    odd = lax.rem(col, 2)
-    beside = col + 1 - 2 * odd
+    even = 1 - lax.rem(col, 2)
+    beside = col - 1 + 2 * even
     ahead = lax.rem(col + 2, n_col)
     behind = lax.rem(col + n_col - 2, n_col)
-    shift_to = ahead + odd * (behind - ahead)
+    shift_to = ahead + even * (behind - ahead)
     has_prev, has_next = place > 0, place < n_line - 1
+    early = RELAYED * (depth // 8)
+    early_rows = pl.ds(0, early)
 
     def line_row(k):
         return lax.rem(row + 2 * k, n_row)
 
-    def piece(i, count):
-        return pl.ds(i * (depth // count), depth // count)
+    def piece(i, count, first=0, last=None):
+        size = ((depth if last is None else last) - first) // count
+        return pl.ds(first + i * size, size)
 
     loads = []
     for i in range(LOADS):
@@ -207,19 +209,14 @@
         pending.append(copy)
         return copy
 
-    def start_swap(i, refs):
-        rows = piece(i, SWAPS)
-        return [
-            start(
-                remote(
-                    ref.at[rows], swapped.at[which, rows],
-                    swap_send.at[which, i], swap_recv.at[which, i], row, beside,
-                )
-            )
-            for which, ref in enumerate(refs)
-        ]
-
-    swaps = [start_swap(i, (upper_hbm, lower_hbm)) for i in range(EARLY)]
+    relays = [
+        start(
+            remote(
+                ref.at[early_rows], relayed.at[which], relay_send.at[which], relay_recv.at[which], row, shift_to
+            )
+        )
+        for which, ref in enumerate((upper_hbm, lower_hbm))
+    ]
 
     def put_statistics(index, g, upper_sums, lower_sums):
         which = lax.broadcasted_iota(jnp.int32, (8, width), 0)
@@ -240,20 +237,16 @@
                     )
                 )
             )
-
-        def finish_line():
-            total = own
-            for k in range(1, n_line):
-                copies[k - 1].wait_recv()
-                total = total + line_in[index, k - 1]
-            return total
-
-        return finish_line
-
-    def pair_copy(index):
-        return remote(
-            totals.at[index, core], totals.at[index, core],
-            pair_send.at[index], pair_recv.at[index], partner, col,
+        total = own
+        for k in range(1, n_line):
+            copies[k - 1].wait_recv()
+            total = total + line_in[index, k - 1]
+        totals[index, core] = total
+        return start(
+            remote(
+                totals.at[index, core], totals.at[index, core],
+                pair_send.at[index], pair_recv.at[index], partner, col,
+            )
         )
 
     def coupling(both_halves, norm_rows):
@@ -279,25 +272,17 @@
         return loaded[0, rows, :], loaded[1, rows, :]
 
     statistics(0, [piece(i, LOADS) for i in range(LOADS)], fetch_loaded)
-
-    for k in range(2):
-        start(
-            remote(
-                gram_out.at[0, k], gram_in.at[core], gram_send.at[k], gram_recv.at[core],
-                chip_row + k, beside,
-            )
-        )
-    swaps += [start_swap(i, (loaded.at[0], loaded.at[1])) for i in range(EARLY, SWAPS)]
+    copy = start(
+        remote(gram_out.at[0, 1 - core], gram_in.at[2], gram_send.at[2], gram_recv.at[2], partner, col)
+    )
 
     for s in range(n_line - 2):
-        tell_up = jnp.logical_and(has_next, place > s)
-        tell_down = jnp.logical_and(has_prev, place < n_line - 1 - s)
-
-        @pl.when(tell_up)
+
+        @pl.when(jnp.logical_and(has_next, place > s))
         def _():
             pl.semaphore_signal(up_sem.at[s], inc=1, device_id={"row": row + 2, "col": col}, device_id_type=MESH)
 
-        @pl.when(tell_down)
+        @pl.when(jnp.logical_and(has_prev, place < n_line - 1 - s))
         def _():
             pl.semaphore_signal(down_sem.at[s], inc=1, device_id={"row": row - 2, "col": col}, device_id_type=MESH)
 
@@ -309,31 +294,8 @@
         def _():
             pl.semaphore_wait(down_sem.at[s], 1)
 
-    for k in range(2):
-        remote(
-            gram_out.at[0, k], gram_in.at[k], gram_send.at[k], gram_recv.at[k], row, beside
-        ).wait_recv()
-    finish_line = reduce_line(0, gram_in[0] + gram_in[1])
-
-    relays = []
-
-    def relay(i):
-        rows = piece(i, SWAPS)
-        for which in range(2):
-            swaps[i][which].wait_recv()
-            relays.append(
-                start(
-                    remote(
-                        swapped.at[which, rows], relayed.at[which, rows],
-                        relay_send.at[which, i], relay_recv.at[which, i], row, shift_to,
-                    )
-                )
-            )
-
-    for i in range(RELAYS_FIRST):
-        relay(i)
-    totals[0, core] = finish_line()
-    own_copy = start(pair_copy(0))
+    copy.wait_recv()
+    own_copy = reduce_line(0, gram_out[0, core] + gram_in[2])
     for k in range(2):
         start(
             remote(
@@ -341,73 +303,87 @@
                 chip_row + k, shift_to,
             )
         )
-    for i in range(RELAYS_FIRST, RELAYS):
-        relay(i)
     own_copy.wait_recv()
     p = coupling(totals[0, :, :half, :], totals[0, 0, half:, :])
-    early_rows = pl.ds(0, RELAYS * (depth // SWAPS))
-    back = wide(p.T)
-    d = swapped[0, early_rows, :] - tall_dot(swapped[1, early_rows, :], back)
+    upper, lower = loaded[0], loaded[1]
+    d = upper - tall_dot(lower, wide(p.T))
     x_wide, p_wide = wide(2.0 * inverse(p)), wide(p)
-    upper_slot, lower_slot = 2 - 2 * odd, 1 + odd
-
-    late = depth - RELAYS * (depth // SWAPS)
+    upper_slot, lower_slot = 2 - 2 * even, 1 + even
+    kept, received = 1 - even, even
+
+    def place_turned(rows, size):
+        new_upper, new_lower = turn(
+            loaded[0, rows, :], loaded[1, rows, :], x_wide, p_wide, d[rows.start : rows.start + size]
+        )
+        home[upper_slot, rows, :] = new_upper
+        home[lower_slot, rows, :] = new_lower
+
+    moves = []
+
+    def move(slot, rows):
+        i = len(moves)
+        moves.append(
+            start(
+                remote(
+                    home.at[slot, rows], work.at[slot, rows], move_send.at[i], move_recv.at[i], row, beside
+                )
+            )
+        )
+
     shifts = []
-    shift_rows = []
-    ready = RELAYS
-    for i in range(SHIFTS):
-        rows = pl.ds(depth - late + i * (late // SHIFTS), late // SHIFTS)
-        shift_rows.append(rows)
-        while ready * (depth // SWAPS) < depth - late + (i + 1) * (late // SHIFTS):
-            swaps[ready][0].wait_recv()
-            swaps[ready][1].wait_recv()
-            ready += 1
-        upper, lower = swapped[0, rows, :], swapped[1, rows, :]
-        new_upper, new_lower = turn(upper, lower, x_wide, p_wide, upper - tall_dot(lower, back))
-        work[upper_slot, rows, :] = new_upper
-        work[lower_slot, rows, :] = new_lower
+    shift_rows = [piece(i, SHIFTS, early) for i in range(SHIFTS)]
+    for i, rows in enumerate(shift_rows):
+        place_turned(rows, rows.size)
         shifts.append(
             start(
                 remote(
-                    work.at[2, rows], work.at[odd, rows], shift_send.at[i], shift_recv.at[i],
+                    home.at[2, rows], home.at[received, rows], shift_send.at[i], shift_recv.at[i],
                     row, shift_to,
                 )
             )
         )
-    if RELAYS:
-        upper, lower = swapped[0, early_rows, :], swapped[1, early_rows, :]
-        new_upper, new_lower = turn(upper, lower, x_wide, p_wide, d)
-        work[upper_slot, early_rows, :] = new_upper
-        work[lower_slot, early_rows, :] = new_lower
-        for k in range(2):
-            remote(
-                totals.at[0, k], others.at[k], other_send.at[k], other_recv.at[k], row, shift_to
-            ).wait_recv()
-        p = coupling(others[:, :half, :], others[0, half:, :])
-        for copy in relays:
-            copy.wait_recv()
-        upper, lower = relayed[0], relayed[1]
-        d = upper - tall_dot(lower, wide(p.T))
-        new_upper, new_lower = turn(upper, lower, wide(2.0 * inverse(p)), wide(p), d)
-        work[2 * odd, early_rows, :] = new_upper
-        work[2 - odd, early_rows, :] = new_lower
+    place_turned(early_rows, early)
+    for i in range(MOVES_FIRST):
+        move(kept, piece(i, MOVES))
+    for k in range(2):
+        remote(
+            totals.at[0, k], others.at[k], other_send.at[k], other_recv.at[k], row, shift_to
+        ).wait_recv()
+    p = coupling(others[:, :half, :], others[0, half:, :])
+    for copy in relays:
+        copy.wait_recv()
+    upper, lower = relayed[0], relayed[1]
+    d = upper - tall_dot(lower, wide(p.T))
+    new_upper, new_lower = turn(upper, lower, wide(2.0 * inverse(p)), wide(p), d)
+    home[2 * even, early_rows, :] = new_upper
+    home[2 - even, early_rows, :] = new_lower
 
     def fetch_shifted(i, rows):
-        if i >= len(pieces) - SHIFTS:
-            shifts[i - (len(pieces) - SHIFTS)].wait_recv()
-        return work[0, rows, :], work[1, rows, :]
-
-    pieces = ([early_rows] if RELAYS else []) + shift_rows
-    statistics(1, pieces, fetch_shifted)
+        if i > 0:
+            shifts[i - 1].wait_recv()
+        return home[0, rows, :], home[1, rows, :]
+
+    statistics(1, [early_rows] + shift_rows, fetch_shifted)
     copy = start(
-        remote(gram_out.at[1, 1 - core], gram_in.at[2], gram_send.at[2], gram_recv.at[2], partner, col)
+        remote(gram_out.at[1, 1 - core], gram_in.at[2], gram_send.at[0], gram_recv.at[0], partner, col)
     )
     copy.wait_recv()
-    total = reduce_line(1, gram_out[1, core] + gram_in[2])()
-    totals[1, core] = total
-    copy = start(pair_copy(1))
-    copy.wait_recv()
+    gram_in[0] = gram_out[1, core] + gram_in[2]
+    crossed = start(remote(gram_in.at[0], gram_in.at[1], gram_send.at[1], gram_recv.at[1], row, beside))
+    for i in range(MOVES_FIRST, MOVES):
+        move(kept, piece(i, MOVES))
+    for i in range(MOVES):
+        move(received, piece(i, MOVES))
+    crossed.wait_recv()
+    reduce_line(1, gram_in[1]).wait_recv()
     out_p[...] = coupling(totals[1, :, :half, :], totals[1, 0, half:, :])
+    incoming = [(received, i) for i in range(MOVES_FIRST)] + [(received, i) for i in range(MOVES_FIRST, MOVES)]
+    incoming += [(kept, i) for i in range(MOVES)]
+    for i, (slot, k) in enumerate(incoming):
+        rows = piece(k, MOVES)
+        remote(
+            home.at[slot, rows], work.at[slot, rows], move_send.at[i], move_recv.at[i], row, beside
+        ).wait_recv()
     for copy in pending:
         copy.wait_send()
 
@@ -439,21 +415,19 @@
     flag = pltpu.SemaphoreType.REGULAR
     work, p = pl.pallas_call(
         functools.partial(kernel, n_row, n_col),
-        out_shape=(pltpu.VMEM((3, depth, width), F32), pltpu.VMEM((width, width), F32)),
+        out_shape=(pltpu.VMEM((2, depth, width), F32), pltpu.VMEM((width, width), F32)),
         in_specs=[pl.BlockSpec(memory_space=pl.ANY)] * 2,
         out_specs=(pl.BlockSpec(memory_space=pltpu.VMEM),) * 2,
         scratch_shapes=[
             pltpu.VMEM((2, depth, width), F32),
-            pltpu.VMEM((2, depth, width), F32),
-            pltpu.VMEM((2, max(RELAYS, 1) * (depth // SWAPS), width), F32),
+            pltpu.VMEM((2, RELAYED * (depth // 8), width), F32),
+            pltpu.VMEM((3, depth, width), F32),
             pltpu.VMEM((ROUNDS, 2, half + 8, width), F32),
             pltpu.VMEM((3, half + 8, width), F32),
             pltpu.VMEM((ROUNDS, half + 8, width), F32),
             pltpu.VMEM((ROUNDS, n_line - 1, half + 8, width), F32),
             pltpu.VMEM((ROUNDS, 2, half + 8, width), F32),
             pltpu.VMEM((2, half + 8, width), F32),
-            dma((2, SWAPS)),
-            dma((2, SWAPS)),
             dma((3,)),
             dma((3,)),
             dma((ROUNDS, n_line - 1)),
@@ -462,10 +436,12 @@
             dma((ROUNDS,)),
             dma((2,)),
             dma((2,)),
-            dma((2, max(RELAYS, 1))),
-            dma((2, max(RELAYS, 1))),
+            dma((2,)),
+            dma((2,)),
             dma((SHIFTS,)),
             dma((SHIFTS,)),
+            dma((2 * MOVES,)),
+            dma((2 * MOVES,)),
             dma((2, LOADS)),
             flag((max(n_line - 2, 1),)),
             flag((max(n_line - 2, 1),)),

time: 35.1 us -> 32.9 us (0.937)
  Pallas kernels: 34.2 us -> 32.3 us
    pallas_call x1, Pallas kernels: 31.4 us -> 29.3 us  [shards(): pl.pallas_call(functools.partial(kernel, n_row, n_col), out_shape=(pltpu....]
where the time goes in v2:
time: 32.9 us
  Pallas kernels  32.3 us (98%)
  between operations  0.64 us (2%)
    pallas_call x1, Pallas kernels, shards(): pl.pallas_call(functools.partial(kernel, n_row, n_col), out_shape=(pltpu....  29.3 us
    pallas_call x1, Pallas kernels, shards(): pl.pallas_call(finish, out_shape=(out, out), in_specs=[pl.BlockSpec(memor...  2.98 us

profile of v2, /device:TPU:1, one launch (start us, length us, event | category | flops | bytes accessed | tf_op | source)
XLA Modules:
  0.0 32.9 jit_solution(10746037709242577999)
XLA Ops:
  0.6 29.3 %shard_map.41 = (f32[2,512,128]{2,1,0:T(8,128)S(1)}, f32[128,128]{1,0:T(8,128)S(1)}) custom-call(f32[512,128]{1,0:T(8,128)} %upper_hbm.1, f32[512,128]{1,0:T(8,128)} %lower_hbm.1), custom_call_target="tpu_custom_call" | custom-call | tf_op jit(solution)/shard_map/pallas_call | solution.py:416
  29.9 3.0 %shard_map.42 = (f32[512,128]{1,0:T(8,128)}, f32[512,128]{1,0:T(8,128)}) custom-call(f32[2,512,128]{2,1,0:T(8,128)S(1)} %get-tuple-element.4.work, f32[128,128]{1,0:T(8,128)S(1)} %get-tuple-element.5.p_ref), custom_call_target="tpu_custom_call" | custom-call | tf_op jit(solution)/shard_map/pallas_call | solution.py:451

commit v3 on v2

--- a/solution.py
+++ b/solution.py
@@ -10,9 +10,11 @@
 ROUNDS = 2
 LOADS = 2
 RELAYED = 5
-SHIFTS = 3
-MOVES = 4
-MOVES_FIRST = 4
+RAW_FROM = 2
+RECEIVED_FIRST = 3
+SHIFTS = 1
+MIDDLE = 4
+EXACT_ABOVE = 1.0
 STORES = 4
 MESH = pl.DeviceIdType.MESH
 F32 = jnp.float32
@@ -83,13 +85,22 @@
     square = (width / 4.0) ** 2
     spread = 0.5 * square / (1.0 + 0.5 * square)
     steps = 0
-    while spread > 3e-6:
+    while spread > 1e-3:
         spread = shrink(spread)[1]
         steps += 1
     return steps
 
 
-def inverse(p):
+def quick_dot(a, b):
+    return tall_dot(a, wide(b))
+
+
+def correct(s, x):
+    e = (identity(x.shape[0]) - x) - exact_dot(s, x)
+    return x + quick_dot(x, e)
+
+
+def inverse_first(p, middle):
     width = p.shape[0]
     eye = identity(width)
     s = exact_dot(p, p.T)
@@ -98,17 +109,30 @@
     scale = 1.0 / (1.0 + 0.5 * total)
     spread = 0.5 * total * scale
     e = spread * eye - scale * s
-    x = None
-    steps = step_count(width)
-    for step in range(steps):
+    gain, spread = shrink(spread)
+    x = (gain * scale) * (eye + e)
+    e = gain * quick_dot(e, e) - spread * eye
+    return inverse_steps((s, x, e, spread), 1, middle, step_count(width))
+
+
+def inverse_steps(state, first, last, steps):
+    s, x, e, spread = state
+    for step in range(first, last):
         gain, spread = shrink(spread)
-        if step == 0:
-            x = (gain * scale) * (eye + e)
-        else:
-            x = gain * (x + exact_dot(x, e))
+        x = gain * (x + quick_dot(x, e))
         if step < steps - 1:
-            e = gain * exact_dot(e, e) - spread * eye
-    return x
+            e = gain * quick_dot(e, e) - spread * identity(x.shape[0])
+    return s, x, e, spread
+
+
+def inverse_last(state, middle):
+    steps = step_count(state[0].shape[0])
+    s, x, _, _ = inverse_steps(state, middle, steps, steps)
+    return correct(s, x)
+
+
+def inverse(p):
+    return inverse_last(inverse_first(p, 1), 1)
 
 
 def inverse_adaptive(p):
@@ -129,7 +153,8 @@
         gain, spread = shrink(spread)
         return gain * (x + exact_dot(x, e)), exact_dot(e, e), gain, spread
 
-    return lax.while_loop(lambda state: state[3] > 3e-6, body, (x, squared, gain, spread))[0]
+    x = lax.while_loop(lambda state: state[3] > 3e-6, body, (x, squared, gain, spread))[0]
+    return lax.cond(bound > EXACT_ABOVE, lambda: correct(s, x), lambda: x)
 
 
 def turn(upper, lower, x_wide, p_wide, d):
@@ -139,10 +164,10 @@
 
 def kernel(
     n_row, n_col, upper_hbm, lower_hbm, work, out_p,
-    loaded, relayed, home, gram_out, gram_in, line_out, line_in, totals, others,
-    gram_send, gram_recv, line_send, line_recv,
-    pair_send, pair_recv, other_send, other_recv, relay_send, relay_recv,
-    shift_send, shift_recv, move_send, move_recv, load_sem, up_sem, down_sem,
+    loaded, relayed, swapped, home, gram_out, gram_in, line_out, line_in, cross_in, totals, others, besides,
+    gram_send, gram_recv, line_send, line_recv, cross_send, cross_recv,
+    pair_send, pair_recv, other_send, other_recv, beside_send, beside_recv,
+    relay_send, relay_recv, swap_send, swap_recv, shift_send, shift_recv, carry_send, carry_recv, move_send, move_recv, load_sem, up_sem, down_sem,
 ):
     depth, width = upper_hbm.shape
     half = width // 2
@@ -153,11 +178,13 @@
     chip_row = row - core
     place = chip_row // 2
     partner = chip_row + 1 - core
-    even = 1 - lax.rem(col, 2)
-    beside = col - 1 + 2 * even
+    odd = lax.rem(col, 2)
+    even = 1 - odd
+    beside = col + 1 - 2 * odd
     ahead = lax.rem(col + 2, n_col)
     behind = lax.rem(col + n_col - 2, n_col)
     shift_to = ahead + even * (behind - ahead)
+    carry_to = ahead + odd * (behind - ahead)
     has_prev, has_next = place > 0, place < n_line - 1
     early = RELAYED * (depth // 8)
     early_rows = pl.ds(0, early)
@@ -209,14 +236,21 @@
         pending.append(copy)
         return copy
 
-    relays = [
-        start(
-            remote(
-                ref.at[early_rows], relayed.at[which], relay_send.at[which], relay_recv.at[which], row, shift_to
-            )
-        )
-        for which, ref in enumerate((upper_hbm, lower_hbm))
-    ]
+    def send_raw(i, first, last, dst, send, recv, c):
+        rows = pl.ds(first * (depth // 8), (last - first) * (depth // 8))
+        return [
+            start(remote(ref.at[rows], dst.at[which, rows], send.at[which, i], recv.at[which, i], row, c))
+            for which, ref in enumerate((upper_hbm, lower_hbm))
+        ]
+
+    def relay(i, first, last):
+        return send_raw(i, first, last, relayed, relay_send, relay_recv, shift_to)
+
+    def swap(i, first, last):
+        return send_raw(i, first, last, swapped, swap_send, swap_recv, beside)
+
+    relays = relay(0, 0, RELAYED)
+    swaps = swap(0, RAW_FROM, 8)
 
     def put_statistics(index, g, upper_sums, lower_sums):
         which = lax.broadcasted_iota(jnp.int32, (8, width), 0)
@@ -225,29 +259,32 @@
             gram_out[index, k, :half, :] = g[k * half : (k + 1) * half]
             gram_out[index, k, half:, :] = norms
 
-    def reduce_line(index, own):
-        line_out[index] = own
+    def share(index, total):
+        totals[index, core] = total
+        return start(
+            remote(
+                totals.at[index, core], totals.at[index, core],
+                pair_send.at[index], pair_recv.at[index], partner, col,
+            )
+        )
+
+    def reduce_line(own):
+        line_out[0] = own
         copies = []
         for k in range(1, n_line):
             copies.append(
                 start(
                     remote(
-                        line_out.at[index], line_in.at[index, k - 1],
-                        line_send.at[index, k - 1], line_recv.at[index, k - 1], line_row(k), col,
+                        line_out.at[0], line_in.at[k - 1],
+                        line_send.at[k - 1], line_recv.at[k - 1], line_row(k), col,
                     )
                 )
             )
         total = own
         for k in range(1, n_line):
             copies[k - 1].wait_recv()
-            total = total + line_in[index, k - 1]
-        totals[index, core] = total
-        return start(
-            remote(
-                totals.at[index, core], totals.at[index, core],
-                pair_send.at[index], pair_recv.at[index], partner, col,
-            )
-        )
+            total = total + line_in[k - 1]
+        return total
 
     def coupling(both_halves, norm_rows):
         norms = norm_rows / row_total
@@ -273,7 +310,7 @@
 
     statistics(0, [piece(i, LOADS) for i in range(LOADS)], fetch_loaded)
     copy = start(
-        remote(gram_out.at[0, 1 - core], gram_in.at[2], gram_send.at[2], gram_recv.at[2], partner, col)
+        remote(gram_out.at[0, 1 - core], gram_in.at[0], gram_send.at[0], gram_recv.at[0], partner, col)
     )
 
     for s in range(n_line - 2):
@@ -295,7 +332,7 @@
             pl.semaphore_wait(down_sem.at[s], 1)
 
     copy.wait_recv()
-    own_copy = reduce_line(0, gram_out[0, core] + gram_in[2])
+    own_copy = share(0, reduce_line(gram_out[0, core] + gram_in[0]))
     for k in range(2):
         start(
             remote(
@@ -303,13 +340,19 @@
                 chip_row + k, shift_to,
             )
         )
+    for k in range(2):
+        start(
+            remote(
+                totals.at[0, core], besides.at[core], beside_send.at[k], beside_recv.at[core],
+                chip_row + k, beside,
+            )
+        )
     own_copy.wait_recv()
     p = coupling(totals[0, :, :half, :], totals[0, 0, half:, :])
     upper, lower = loaded[0], loaded[1]
     d = upper - tall_dot(lower, wide(p.T))
     x_wide, p_wide = wide(2.0 * inverse(p)), wide(p)
     upper_slot, lower_slot = 2 - 2 * even, 1 + even
-    kept, received = 1 - even, even
 
     def place_turned(rows, size):
         new_upper, new_lower = turn(
@@ -318,16 +361,15 @@
         home[upper_slot, rows, :] = new_upper
         home[lower_slot, rows, :] = new_lower
 
-    moves = []
-
-    def move(slot, rows):
-        i = len(moves)
-        moves.append(
-            start(
-                remote(
-                    home.at[slot, rows], work.at[slot, rows], move_send.at[i], move_recv.at[i], row, beside
-                )
-            )
+    def eighths(first, last):
+        return pl.ds(first * (depth // 8), (last - first) * (depth // 8))
+
+    move_rows = [eighths(0, RAW_FROM), eighths(0, RECEIVED_FIRST), eighths(RECEIVED_FIRST, RELAYED)]
+
+    def move_copy(i, slot):
+        return remote(
+            home.at[slot, move_rows[i]], work.at[slot, move_rows[i]],
+            move_send.at[i], move_recv.at[i], row, beside,
         )
 
     shifts = []
@@ -337,14 +379,13 @@
         shifts.append(
             start(
                 remote(
-                    home.at[2, rows], home.at[received, rows], shift_send.at[i], shift_recv.at[i],
+                    home.at[2, rows], home.at[even, rows], shift_send.at[i], shift_recv.at[i],
                     row, shift_to,
                 )
             )
         )
     place_turned(early_rows, early)
-    for i in range(MOVES_FIRST):
-        move(kept, piece(i, MOVES))
+    start(move_copy(0, odd))
     for k in range(2):
         remote(
             totals.at[0, k], others.at[k], other_send.at[k], other_recv.at[k], row, shift_to
@@ -358,6 +399,8 @@
     home[2 * even, early_rows, :] = new_upper
     home[2 - even, early_rows, :] = new_lower
 
+    start(move_copy(1, even))
+
     def fetch_shifted(i, rows):
         if i > 0:
             shifts[i - 1].wait_recv()
@@ -365,25 +408,52 @@
 
     statistics(1, [early_rows] + shift_rows, fetch_shifted)
     copy = start(
-        remote(gram_out.at[1, 1 - core], gram_in.at[2], gram_send.at[0], gram_recv.at[0], partner, col)
+        remote(gram_out.at[1, 1 - core], gram_in.at[1], gram_send.at[1], gram_recv.at[1], partner, col)
     )
+    for k in range(2):
+        remote(
+            totals.at[0, k], besides.at[k], beside_send.at[k], beside_recv.at[k], row, beside
+        ).wait_recv()
+    p = coupling(besides[:, :half, :], besides[0, half:, :])
+    back, p_wide, state = wide(p.T), wide(p), inverse_first(p, MIDDLE)
     copy.wait_recv()
-    gram_in[0] = gram_out[1, core] + gram_in[2]
-    crossed = start(remote(gram_in.at[0], gram_in.at[1], gram_send.at[1], gram_recv.at[1], row, beside))
-    for i in range(MOVES_FIRST, MOVES):
-        move(kept, piece(i, MOVES))
-    for i in range(MOVES):
-        move(received, piece(i, MOVES))
-    crossed.wait_recv()
-    reduce_line(1, gram_in[1]).wait_recv()
+    line_out[1] = gram_out[1, core] + gram_in[1]
+    crossing = [
+        start(
+            remote(
+                line_out.at[1], cross_in.at[k], cross_send.at[k], cross_recv.at[k], line_row(k), beside
+            )
+        )
+        for k in reversed(range(n_line))
+    ]
+    start(move_copy(2, even))
+    x_wide = wide(2.0 * inverse_last(state, MIDDLE))
+    for copy in swaps:
+        copy.wait_recv()
+
+    def place_swapped(rows):
+        upper, lower = swapped[0, rows, :], swapped[1, rows, :]
+        new_upper, new_lower = turn(upper, lower, x_wide, p_wide, upper - tall_dot(lower, back))
+        work[2 - 2 * odd, rows, :] = new_upper
+        work[1 + odd, rows, :] = new_lower
+
+    late_rows = eighths(RELAYED, 8)
+    place_swapped(late_rows)
+    carried = start(
+        remote(
+            work.at[2, late_rows], work.at[odd, late_rows], carry_send.at[0], carry_recv.at[0], row, carry_to
+        )
+    )
+    place_swapped(eighths(RAW_FROM, RELAYED))
+    total = 0.0
+    for k in range(n_line):
+        crossing[n_line - 1 - k].wait_recv()
+        total = total + cross_in[k]
+    share(1, total).wait_recv()
     out_p[...] = coupling(totals[1, :, :half, :], totals[1, 0, half:, :])
-    incoming = [(received, i) for i in range(MOVES_FIRST)] + [(received, i) for i in range(MOVES_FIRST, MOVES)]
-    incoming += [(kept, i) for i in range(MOVES)]
-    for i, (slot, k) in enumerate(incoming):
-        rows = piece(k, MOVES)
-        remote(
-            home.at[slot, rows], work.at[slot, rows], move_send.at[i], move_recv.at[i], row, beside
-        ).wait_recv()
+    carried.wait_recv()
+    for i, slot in enumerate((even, odd, odd)):
+        move_copy(i, slot).wait_recv()
     for copy in pending:
         copy.wait_send()
 
@@ -415,33 +485,44 @@
     flag = pltpu.SemaphoreType.REGULAR
     work, p = pl.pallas_call(
         functools.partial(kernel, n_row, n_col),
-        out_shape=(pltpu.VMEM((2, depth, width), F32), pltpu.VMEM((width, width), F32)),
+        out_shape=(pltpu.VMEM((3, depth, width), F32), pltpu.VMEM((width, width), F32)),
         in_specs=[pl.BlockSpec(memory_space=pl.ANY)] * 2,
         out_specs=(pl.BlockSpec(memory_space=pltpu.VMEM),) * 2,
         scratch_shapes=[
             pltpu.VMEM((2, depth, width), F32),
             pltpu.VMEM((2, RELAYED * (depth // 8), width), F32),
+            pltpu.VMEM((2, depth, width), F32),
             pltpu.VMEM((3, depth, width), F32),
             pltpu.VMEM((ROUNDS, 2, half + 8, width), F32),
-            pltpu.VMEM((3, half + 8, width), F32),
+            pltpu.VMEM((2, half + 8, width), F32),
             pltpu.VMEM((ROUNDS, half + 8, width), F32),
-            pltpu.VMEM((ROUNDS, n_line - 1, half + 8, width), F32),
+            pltpu.VMEM((n_line - 1, half + 8, width), F32),
+            pltpu.VMEM((n_line, half + 8, width), F32),
             pltpu.VMEM((ROUNDS, 2, half + 8, width), F32),
             pltpu.VMEM((2, half + 8, width), F32),
-            dma((3,)),
-            dma((3,)),
-            dma((ROUNDS, n_line - 1)),
-            dma((ROUNDS, n_line - 1)),
+            pltpu.VMEM((2, half + 8, width), F32),
+            dma((2,)),
+            dma((2,)),
+            dma((n_line - 1,)),
+            dma((n_line - 1,)),
+            dma((n_line,)),
+            dma((n_line,)),
             dma((ROUNDS,)),
             dma((ROUNDS,)),
             dma((2,)),
             dma((2,)),
             dma((2,)),
             dma((2,)),
+            dma((2, 2)),
+            dma((2, 2)),
+            dma((2, 2)),
+            dma((2, 2)),
             dma((SHIFTS,)),
             dma((SHIFTS,)),
-            dma((2 * MOVES,)),
-            dma((2 * MOVES,)),
+            dma((1,)),
+            dma((1,)),
+            dma((3,)),
+            dma((3,)),
             dma((2, LOADS)),
             flag((max(n_line - 2, 1),)),
             flag((max(n_line - 2, 1),)),

time: 32.9 us -> 32.4 us (0.985)
  Pallas kernels: 32.3 us -> 31.5 us
    pallas_call x1, Pallas kernels: 29.3 us -> 28.4 us  [shards(): pl.pallas_call(functools.partial(kernel, n_row, n_col), out_shape=(pltpu....]
where the time goes in v3:
time: 32.4 us; the launch traced here: 32.1 us
  Pallas kernels  31.5 us (97%)
  between operations  0.64 us (2%)
    pallas_call x1, Pallas kernels, shards(): pl.pallas_call(functools.partial(kernel, n_row, n_col), out_shape=(pltpu....  28.4 us
    pallas_call x1, Pallas kernels, shards(): pl.pallas_call(finish, out_shape=(out, out), in_specs=[pl.BlockSpec(memor...  3.12 us

profile of v3, /device:TPU:1, one launch (start us, length us, event | category | flops | bytes accessed | tf_op | source)
XLA Modules:
  0.0 32.1 jit_solution(17303339093388658895)
XLA Ops:
  0.6 28.4 %shard_map.41 = (f32[3,512,128]{2,1,0:T(8,128)S(1)}, f32[128,128]{1,0:T(8,128)S(1)}) custom-call(f32[512,128]{1,0:T(8,128)} %upper_hbm.1, f32[512,128]{1,0:T(8,128)} %lower_hbm.1), custom_call_target="tpu_custom_call" | custom-call | tf_op jit(solution)/shard_map/pallas_call | solution.py:486
  29.0 3.1 %shard_map.42 = (f32[512,128]{1,0:T(8,128)}, f32[512,128]{1,0:T(8,128)}) custom-call(f32[3,512,128]{2,1,0:T(8,128)S(1)} %get-tuple-element.4.work, f32[128,128]{1,0:T(8,128)S(1)} %get-tuple-element.5.p_ref), custom_call_target="tpu_custom_call" | custom-call | tf_op jit(solution)/shard_map/pallas_call | solution.py:532

commit v4 on v3

--- a/solution.py
+++ b/solution.py
@@ -13,7 +13,6 @@
 RAW_FROM = 2
 RECEIVED_FIRST = 3
 SHIFTS = 1
-MIDDLE = 4
 EXACT_ABOVE = 1.0
 STORES = 4
 MESH = pl.DeviceIdType.MESH
@@ -100,7 +99,7 @@
     return x + quick_dot(x, e)
 
 
-def inverse_first(p, middle):
+def inverse(p):
     width = p.shape[0]
     eye = identity(width)
     s = exact_dot(p, p.T)
@@ -109,30 +108,17 @@
     scale = 1.0 / (1.0 + 0.5 * total)
     spread = 0.5 * total * scale
     e = spread * eye - scale * s
-    gain, spread = shrink(spread)
-    x = (gain * scale) * (eye + e)
-    e = gain * quick_dot(e, e) - spread * eye
-    return inverse_steps((s, x, e, spread), 1, middle, step_count(width))
-
-
-def inverse_steps(state, first, last, steps):
-    s, x, e, spread = state
-    for step in range(first, last):
+    x = None
+    steps = step_count(width)
+    for step in range(steps):
         gain, spread = shrink(spread)
-        x = gain * (x + quick_dot(x, e))
+        if step == 0:
+            x = (gain * scale) * (eye + e)
+        else:
+            x = gain * (x + quick_dot(x, e))
         if step < steps - 1:
-            e = gain * quick_dot(e, e) - spread * identity(x.shape[0])
-    return s, x, e, spread
-
-
-def inverse_last(state, middle):
-    steps = step_count(state[0].shape[0])
-    s, x, _, _ = inverse_steps(state, middle, steps, steps)
+            e = gain * quick_dot(e, e) - spread * eye
     return correct(s, x)
-
-
-def inverse(p):
-    return inverse_last(inverse_first(p, 1), 1)
 
 
 def inverse_adaptive(p):
@@ -410,12 +396,6 @@
     copy = start(
         remote(gram_out.at[1, 1 - core], gram_in.at[1], gram_send.at[1], gram_recv.at[1], partner, col)
     )
-    for k in range(2):
-        remote(
-            totals.at[0, k], besides.at[k], beside_send.at[k], beside_recv.at[k], row, beside
-        ).wait_recv()
-    p = coupling(besides[:, :half, :], besides[0, half:, :])
-    back, p_wide, state = wide(p.T), wide(p), inverse_first(p, MIDDLE)
     copy.wait_recv()
     line_out[1] = gram_out[1, core] + gram_in[1]
     crossing = [
@@ -427,7 +407,12 @@
         for k in reversed(range(n_line))
     ]
     start(move_copy(2, even))
-    x_wide = wide(2.0 * inverse_last(state, MIDDLE))
+    for k in range(2):
+        remote(
+            totals.at[0, k], besides.at[k], beside_send.at[k], beside_recv.at[k], row, beside
+        ).wait_recv()
+    p = coupling(besides[:, :half, :], besides[0, half:, :])
+    back, p_wide, x_wide = wide(p.T), wide(p), wide(2.0 * inverse(p))
     for copy in swaps:
         copy.wait_recv()
 

time: 32.4 us -> 31.5 us (0.972)
  Pallas kernels: 31.5 us -> 30.7 us
    pallas_call x1, Pallas kernels: 28.4 us -> 27.4 us  [shards(): pl.pallas_call(functools.partial(kernel, n_row, n_col), out_shape=(pltpu....]
where the time goes in v4:
time: 31.5 us; the launch traced here: 31.4 us
  Pallas kernels  30.7 us (97%)
  between operations  0.64 us (2%)
    pallas_call x1, Pallas kernels, shards(): pl.pallas_call(functools.partial(kernel, n_row, n_col), out_shape=(pltpu....  27.4 us
    pallas_call x1, Pallas kernels, shards(): pl.pallas_call(finish, out_shape=(out, out), in_specs=[pl.BlockSpec(memor...  3.34 us

profile of v4, /device:TPU:1, one launch (start us, length us, event | category | flops | bytes accessed | tf_op | source)
XLA Modules:
  0.0 31.4 jit_solution(15562213344922719493)
XLA Ops:
  0.6 27.4 %shard_map.41 = (f32[3,512,128]{2,1,0:T(8,128)S(1)}, f32[128,128]{1,0:T(8,128)S(1)}) custom-call(f32[512,128]{1,0:T(8,128)} %upper_hbm.1, f32[512,128]{1,0:T(8,128)} %lower_hbm.1), custom_call_target="tpu_custom_call" | custom-call | tf_op jit(solution)/shard_map/pallas_call | solution.py:471
  28.0 3.3 %shard_map.42 = (f32[512,128]{1,0:T(8,128)}, f32[512,128]{1,0:T(8,128)}) custom-call(f32[3,512,128]{2,1,0:T(8,128)S(1)} %get-tuple-element.4.work, f32[128,128]{1,0:T(8,128)S(1)} %get-tuple-element.5.p_ref), custom_call_target="tpu_custom_call" | custom-call | tf_op jit(solution)/shard_map/pallas_call | solution.py:517

commit v5 on v4

--- a/solution.py
+++ b/solution.py
@@ -8,8 +8,9 @@
 from jax.sharding import PartitionSpec as P
 
 ROUNDS = 2
-LOADS = 2
+LOADS = 1
 RELAYED = 5
+RELAYED_FIRST = 5
 RAW_FROM = 2
 RECEIVED_FIRST = 3
 SHIFTS = 1
@@ -128,18 +129,16 @@
     bound = 1.0001 * jnp.max(jnp.sum(jnp.abs(s), axis=0, keepdims=True))
     scale = 1.0 / (1.0 + 0.5 * bound)
     spread = 0.5 * bound * scale
-    e = spread * eye - scale * s
-    gain, spread = shrink(spread)
-    x = (gain * scale) * (eye + e)
-    squared = exact_dot(e, e)
+    squared = (scale * scale) * exact_dot(s, s) + (spread * spread) * eye - (2.0 * spread * scale) * s
+    gain, smaller = shrink(spread)
+    x = (gain * scale) * ((1.0 + spread) * eye - scale * s)
 
     def body(state):
-        x, squared, gain, spread = state
-        e = gain * squared - spread * eye
+        x, e, spread = state
         gain, spread = shrink(spread)
-        return gain * (x + exact_dot(x, e)), exact_dot(e, e), gain, spread
-
-    x = lax.while_loop(lambda state: state[3] > 3e-6, body, (x, squared, gain, spread))[0]
+        return gain * (x + quick_dot(x, e)), gain * quick_dot(e, e) - spread * eye, spread
+
+    x = lax.while_loop(lambda state: state[2] > 3e-6, body, (x, gain * squared - smaller * eye, smaller))[0]
     return lax.cond(bound > EXACT_ABOVE, lambda: correct(s, x), lambda: x)
 
 
@@ -174,6 +173,7 @@
     has_prev, has_next = place > 0, place < n_line - 1
     early = RELAYED * (depth // 8)
     early_rows = pl.ds(0, early)
+    line = pl.ds(0, half + 1)
 
     def line_row(k):
         return lax.rem(row + 2 * k, n_row)
@@ -235,33 +235,31 @@
     def swap(i, first, last):
         return send_raw(i, first, last, swapped, swap_send, swap_recv, beside)
 
-    relays = relay(0, 0, RELAYED)
+    relays = relay(0, 0, RELAYED_FIRST)
     swaps = swap(0, RAW_FROM, 8)
 
     def put_statistics(index, g, upper_sums, lower_sums):
-        which = lax.broadcasted_iota(jnp.int32, (8, width), 0)
-        norms = jnp.where(which == 0, upper_sums, jnp.where(which == 1, lower_sums, 0.0))
-        for k in range(2):
+        for k, sums in enumerate((upper_sums, lower_sums)):
             gram_out[index, k, :half, :] = g[k * half : (k + 1) * half]
-            gram_out[index, k, half:, :] = norms
+            gram_out[index, k, half : half + 1, :] = sums
 
     def share(index, total):
-        totals[index, core] = total
+        totals[index, core, line, :] = total
         return start(
             remote(
-                totals.at[index, core], totals.at[index, core],
+                totals.at[index, core, line], totals.at[index, core, line],
                 pair_send.at[index], pair_recv.at[index], partner, col,
             )
         )
 
     def reduce_line(own):
-        line_out[0] = own
+        line_out[0, line, :] = own
         copies = []
         for k in range(1, n_line):
             copies.append(
                 start(
                     remote(
-                        line_out.at[0], line_in.at[k - 1],
+                        line_out.at[0, line], line_in.at[k - 1, line],
                         line_send.at[k - 1], line_recv.at[k - 1], line_row(k), col,
                     )
                 )
@@ -269,16 +267,16 @@
         total = own
         for k in range(1, n_line):
             copies[k - 1].wait_recv()
-            total = total + line_in[k - 1]
+            total = total + line_in[k - 1, line, :]
         return total
 
-    def coupling(both_halves, norm_rows):
-        norms = norm_rows / row_total
-        a_row, b = norms[:1], norms[1:2]
+    def coupling(read):
+        both_halves = jnp.concatenate([read(k, slice(0, half)) for k in range(2)], axis=0)
+        a_row, b = (read(k, slice(half, half + 1)) / row_total for k in range(2))
         a = jnp.broadcast_to(a_row, (width, width)).T
         gap, both = a - b, a + b
         factor = -gap / (2.0 * gap * gap + 0.5 * both * both + 1e-05)
-        return (both_halves.reshape(width, width) / row_total) * factor
+        return (both_halves / row_total) * factor
 
     def statistics(index, pieces, fetch):
         g, upper_sums, lower_sums = 0.0, 0.0, 0.0
@@ -296,7 +294,7 @@
 
     statistics(0, [piece(i, LOADS) for i in range(LOADS)], fetch_loaded)
     copy = start(
-        remote(gram_out.at[0, 1 - core], gram_in.at[0], gram_send.at[0], gram_recv.at[0], partner, col)
+        remote(gram_out.at[0, 1 - core, line], gram_in.at[0, line], gram_send.at[0], gram_recv.at[0], partner, col)
     )
 
     for s in range(n_line - 2):
@@ -318,23 +316,25 @@
             pl.semaphore_wait(down_sem.at[s], 1)
 
     copy.wait_recv()
-    own_copy = share(0, reduce_line(gram_out[0, core] + gram_in[0]))
+    own_copy = share(0, reduce_line(gram_out[0, core, line, :] + gram_in[0, line, :]))
     for k in range(2):
         start(
             remote(
-                totals.at[0, core], others.at[core], other_send.at[k], other_recv.at[core],
+                totals.at[0, core, line], others.at[core, line], other_send.at[k], other_recv.at[core],
                 chip_row + k, shift_to,
             )
         )
     for k in range(2):
         start(
             remote(
-                totals.at[0, core], besides.at[core], beside_send.at[k], beside_recv.at[core],
+                totals.at[0, core, line], besides.at[core, line], beside_send.at[k], beside_recv.at[core],
                 chip_row + k, beside,
             )
         )
+    if RELAYED > RELAYED_FIRST:
+        relays += relay(1, RELAYED_FIRST, RELAYED)
     own_copy.wait_recv()
-    p = coupling(totals[0, :, :half, :], totals[0, 0, half:, :])
+    p = coupling(lambda k, rows: totals[0, k, rows, :])
     upper, lower = loaded[0], loaded[1]
     d = upper - tall_dot(lower, wide(p.T))
     x_wide, p_wide = wide(2.0 * inverse(p)), wide(p)
@@ -374,9 +374,9 @@
     start(move_copy(0, odd))
     for k in range(2):
         remote(
-            totals.at[0, k], others.at[k], other_send.at[k], other_recv.at[k], row, shift_to
+            totals.at[0, k, line], others.at[k, line], other_send.at[k], other_recv.at[k], row, shift_to
         ).wait_recv()
-    p = coupling(others[:, :half, :], others[0, half:, :])
+    p = coupling(lambda k, rows: others[k, rows, :])
     for copy in relays:
         copy.wait_recv()
     upper, lower = relayed[0], relayed[1]
@@ -394,14 +394,14 @@
 
     statistics(1, [early_rows] + shift_rows, fetch_shifted)
     copy = start(
-        remote(gram_out.at[1, 1 - core], gram_in.at[1], gram_send.at[1], gram_recv.at[1], partner, col)
+        remote(gram_out.at[1, 1 - core, line], gram_in.at[1, line], gram_send.at[1], gram_recv.at[1], partner, col)
     )
     copy.wait_recv()
-    line_out[1] = gram_out[1, core] + gram_in[1]
+    line_out[1, line, :] = gram_out[1, core, line, :] + gram_in[1, line, :]
     crossing = [
         start(
             remote(
-                line_out.at[1], cross_in.at[k], cross_send.at[k], cross_recv.at[k], line_row(k), beside
+                line_out.at[1, line], cross_in.at[k, line], cross_send.at[k], cross_recv.at[k], line_row(k), beside
             )
         )
         for k in reversed(range(n_line))
@@ -409,9 +409,9 @@
     start(move_copy(2, even))
     for k in range(2):
         remote(
-            totals.at[0, k], besides.at[k], beside_send.at[k], beside_recv.at[k], row, beside
+            totals.at[0, k, line], besides.at[k, line], beside_send.at[k], beside_recv.at[k], row, beside
         ).wait_recv()
-    p = coupling(besides[:, :half, :], besides[0, half:, :])
+    p = coupling(lambda k, rows: besides[k, rows, :])
     back, p_wide, x_wide = wide(p.T), wide(p), wide(2.0 * inverse(p))
     for copy in swaps:
         copy.wait_recv()
@@ -433,9 +433,9 @@
     total = 0.0
     for k in range(n_line):
         crossing[n_line - 1 - k].wait_recv()
-        total = total + cross_in[k]
+        total = total + cross_in[k, line, :]
     share(1, total).wait_recv()
-    out_p[...] = coupling(totals[1, :, :half, :], totals[1, 0, half:, :])
+    out_p[...] = coupling(lambda k, rows: totals[1, k, rows, :])
     carried.wait_recv()
     for i, slot in enumerate((even, odd, odd)):
         move_copy(i, slot).wait_recv()

time: 31.5 us -> 30.6 us (0.971)
  Pallas kernels: 30.7 us -> 29.8 us
    pallas_call x1, Pallas kernels: 3.34 us -> 2.86 us  [shards(): pl.pallas_call(finish, out_shape=(out, out), in_specs=[pl.BlockSpec(memor...]
    pallas_call x1, Pallas kernels: 27.4 us -> 26.9 us  [shards(): pl.pallas_call(functools.partial(kernel, n_row, n_col), out_shape=(pltpu....]
where the time goes in v5:
time: 30.6 us; the launch traced here: 30.4 us
  Pallas kernels  29.8 us (97%)
  between operations  0.64 us (2%)
    pallas_call x1, Pallas kernels, shards(): pl.pallas_call(functools.partial(kernel, n_row, n_col), out_shape=(pltpu....  26.9 us
    pallas_call x1, Pallas kernels, shards(): pl.pallas_call(finish, out_shape=(out, out), in_specs=[pl.BlockSpec(memor...  2.86 us

profile of v5, /device:TPU:1, one launch (start us, length us, event | category | flops | bytes accessed | tf_op | source)
XLA Modules:
  0.0 30.4 jit_solution(8139116509843090002)
XLA Ops:
  0.6 26.9 %shard_map.41 = (f32[3,512,128]{2,1,0:T(8,128)S(1)}, f32[128,128]{1,0:T(8,128)S(1)}) custom-call(f32[512,128]{1,0:T(8,128)} %upper_hbm.1, f32[512,128]{1,0:T(8,128)} %lower_hbm.1), custom_call_target="tpu_custom_call" | custom-call | tf_op jit(solution)/shard_map/pallas_call | solution.py:471
  27.6 2.9 %shard_map.42 = (f32[512,128]{1,0:T(8,128)}, f32[512,128]{1,0:T(8,128)}) custom-call(f32[3,512,128]{2,1,0:T(8,128)S(1)} %get-tuple-element.4.work, f32[128,128]{1,0:T(8,128)S(1)} %get-tuple-element.5.p_ref), custom_call_target="tpu_custom_call" | custom-call | tf_op jit(solution)/shard_map/pallas_call | solution.py:517

commit v6 on v5

--- a/solution.py
+++ b/solution.py
@@ -12,7 +12,7 @@
 RELAYED = 5
 RELAYED_FIRST = 5
 RAW_FROM = 2
-RECEIVED_FIRST = 3
+RECEIVED_FIRST = 4
 SHIFTS = 1
 EXACT_ABOVE = 1.0
 STORES = 4
@@ -404,7 +404,7 @@
                 line_out.at[1, line], cross_in.at[k, line], cross_send.at[k], cross_recv.at[k], line_row(k), beside
             )
         )
-        for k in reversed(range(n_line))
+        for k in range(n_line)
     ]
     start(move_copy(2, even))
     for k in range(2):
@@ -432,7 +432,7 @@
     place_swapped(eighths(RAW_FROM, RELAYED))
     total = 0.0
     for k in range(n_line):
-        crossing[n_line - 1 - k].wait_recv()
+        crossing[k].wait_recv()
         total = total + cross_in[k, line, :]
     share(1, total).wait_recv()
     out_p[...] = coupling(lambda k, rows: totals[1, k, rows, :])

time: 30.6 us -> 30 us (0.980)
  Pallas kernels: 29.8 us -> 29.3 us
    pallas_call x1, Pallas kernels: 26.9 us -> 26.3 us  [shards(): pl.pallas_call(functools.partial(kernel, n_row, n_col), out_shape=(pltpu....]
where the time goes in v6:
time: 30 us
  Pallas kernels  29.3 us (98%)
  between operations  0.64 us (2%)
    pallas_call x1, Pallas kernels, shards(): pl.pallas_call(functools.partial(kernel, n_row, n_col), out_shape=(pltpu....  26.3 us
    pallas_call x1, Pallas kernels, shards(): pl.pallas_call(finish, out_shape=(out, out), in_specs=[pl.BlockSpec(memor...  3.07 us

profile of v6, /device:TPU:1, one launch (start us, length us, event | category | flops | bytes accessed | tf_op | source)
XLA Modules:
  0.0 30.0 jit_solution(821651205180038991)
XLA Ops:
  0.6 26.3 %shard_map.41 = (f32[3,512,128]{2,1,0:T(8,128)S(1)}, f32[128,128]{1,0:T(8,128)S(1)}) custom-call(f32[512,128]{1,0:T(8,128)} %upper_hbm.1, f32[512,128]{1,0:T(8,128)} %lower_hbm.1), custom_call_target="tpu_custom_call" | custom-call | tf_op jit(solution)/shard_map/pallas_call | solution.py:471
  26.9 3.1 %shard_map.42 = (f32[512,128]{1,0:T(8,128)}, f32[512,128]{1,0:T(8,128)}) custom-call(f32[3,512,128]{2,1,0:T(8,128)S(1)} %get-tuple-element.4.work, f32[128,128]{1,0:T(8,128)S(1)} %get-tuple-element.5.p_ref), custom_call_target="tpu_custom_call" | custom-call | tf_op jit(solution)/shard_map/pallas_call | solution.py:517

commit v7 on v6

--- a/solution.py
+++ b/solution.py
@@ -138,7 +138,8 @@
         gain, spread = shrink(spread)
         return gain * (x + quick_dot(x, e)), gain * quick_dot(e, e) - spread * eye, spread
 
-    x = lax.while_loop(lambda state: state[2] > 3e-6, body, (x, gain * squared - smaller * eye, smaller))[0]
+    state = body((x, gain * squared - smaller * eye, smaller))
+    x = lax.while_loop(lambda state: state[2] > 3e-6, body, state)[0]
     return lax.cond(bound > EXACT_ABOVE, lambda: correct(s, x), lambda: x)
 
 
@@ -321,14 +322,14 @@
         start(
             remote(
                 totals.at[0, core, line], others.at[core, line], other_send.at[k], other_recv.at[core],
-                chip_row + k, shift_to,
+                (row, partner)[k], shift_to,
             )
         )
     for k in range(2):
         start(
             remote(
                 totals.at[0, core, line], besides.at[core, line], beside_send.at[k], beside_recv.at[core],
-                chip_row + k, beside,
+                (row, partner)[k], beside,
             )
         )
     if RELAYED > RELAYED_FIRST:

time: 30 us -> 30 us (level)
  no operation moved by 1% of the time
where the time goes in v7:
time: 30 us
  Pallas kernels  29.3 us (98%)
  between operations  0.64 us (2%)
    pallas_call x1, Pallas kernels, shards(): pl.pallas_call(functools.partial(kernel, n_row, n_col), out_shape=(pltpu....  26.3 us
    pallas_call x1, Pallas kernels, shards(): pl.pallas_call(finish, out_shape=(out, out), in_specs=[pl.BlockSpec(memor...  3.06 us

profile of v7, /device:TPU:1, one launch (start us, length us, event | category | flops | bytes accessed | tf_op | source)
XLA Modules:
  0.0 30.0 jit_solution(17984935726869449999)
XLA Ops:
  0.6 26.3 %shard_map.41 = (f32[3,512,128]{2,1,0:T(8,128)S(1)}, f32[128,128]{1,0:T(8,128)S(1)}) custom-call(f32[512,128]{1,0:T(8,128)} %upper_hbm.1, f32[512,128]{1,0:T(8,128)} %lower_hbm.1), custom_call_target="tpu_custom_call" | custom-call | tf_op jit(solution)/shard_map/pallas_call | solution.py:472
  26.9 3.1 %shard_map.42 = (f32[512,128]{1,0:T(8,128)}, f32[512,128]{1,0:T(8,128)}) custom-call(f32[3,512,128]{2,1,0:T(8,128)S(1)} %get-tuple-element.4.work, f32[128,128]{1,0:T(8,128)S(1)} %get-tuple-element.5.p_ref), custom_call_target="tpu_custom_call" | custom-call | tf_op jit(solution)/shard_map/pallas_call | solution.py:518
